TPU v7x, 32 devices: a whole 2x2x4 slice. The times are simulated.
32 devices in a mesh: parts: 2 (over x), seq: 16 (over z, y, core).
Axes of the slice: x: 2, y: 2, z: 4, core: 2. Of those that a mesh axis runs over, the one named last changes fastest.
Arguments:
- tokens: bfloat16 [131072, 512], P(('parts', 'seq')), parts along dimension 0, may hold values from -6 to 6
- w_value: bfloat16 [512, 512], replicated, may hold values from -0.25 to 0.25
- w_gate: bfloat16 [512, 512], replicated, may hold values from -0.25 to 0.25
- first_block: bfloat16 [256, 256], replicated, may hold values from -0.375 to 0.375
- second_block: bfloat16 [256, 256], replicated, may hold values from -0.375 to 0.375
- third_block: bfloat16 [256, 256], replicated, may hold values from -0.375 to 0.375
- fourth_block: bfloat16 [256, 256], replicated, may hold values from -0.375 to 0.375
- kernel: bfloat16 [512, 256, 256], P('seq'), may hold values from -6 to 6
- skip_gain: float32 [512], replicated, may hold values from 0.25 to 2
- cotangent: bfloat16 [131072, 512], P(('parts', 'seq')), parts along dimension 0, may hold values from -6 to 6
Outputs:
- grad_tokens: bfloat16 [131072, 512], P(('parts', 'seq')), parts along dimension 0
- grad_kernel: bfloat16 [1024, 256, 256], P(('parts', 'seq')), parts along dimension 0
- grad_weights: float32 [4, 512, 512], P('parts'), parts along dimension 0
- grad_skip: float32 [1024], P('parts'), parts along dimension 0
There are 2 independent parts, one for each index of `parts`. A program takes and returns all parts, laid end to end along the dimension named above; an argument that names none is the same for every part. Nothing has to cross between parts.
All inputs are finite; a program needn't handle non-finite values.
Results may differ from a plain program's by a relative error of at most 0.025.
Values may be sent and summed in bfloat16 or wider, within the bound.
A program may use at most 128 MiB of HBM per device.

v0:
```python
import jax
import jax.numpy as jnp
from jax import lax
from jax.sharding import PartitionSpec as P

D = 512
N1 = 256
N2 = 256


def on_device(
    tokens,
    w_value,
    w_gate,
    first_block,
    second_block,
    third_block,
    fourth_block,
    kernel,
    skip_gain,
    cotangent,
):
    f32 = jnp.float32
    bf16 = jnp.bfloat16
    n_devices = lax.axis_size("seq")
    rows_here = N1 // n_devices
    local_rows = tokens.shape[0]
    value = jnp.dot(tokens, w_value, preferred_element_type=f32).astype(bf16)
    gate = jnp.dot(tokens, w_gate, preferred_element_type=f32).astype(bf16)
    cube = value.reshape(rows_here, N2, D)
    section_one = jnp.einsum("abc,pb->cap", cube, first_block, preferred_element_type=f32).astype(
        bf16
    )
    spectrum = jnp.einsum(
        "cap,qa->cqp",
        lax.all_to_all(section_one, "seq", split_axis=0, concat_axis=1, tiled=True),
        second_block,
        preferred_element_type=f32,
    )
    filtered = (spectrum * kernel.astype(f32)).astype(bf16)
    section_three = jnp.einsum(
        "cqp,rq->crp", filtered, third_block, preferred_element_type=f32
    ).astype(bf16)
    split_three = section_three.reshape(section_three.shape[0], n_devices, rows_here, N2)
    conv = jnp.einsum(
        "crp,sp->rsc",
        lax.all_to_all(split_three, "seq", split_axis=1, concat_axis=0, tiled=True)[:, 0],
        fourth_block,
        preferred_element_type=f32,
    )
    mixed = conv.reshape(local_rows, D) + skip_gain * value.astype(f32)
    upstream = cotangent.astype(f32)
    d_mix = (upstream * gate.astype(f32)).astype(bf16)
    d_gate = (upstream * mixed).astype(bf16)
    d_mix_cube = d_mix.reshape(rows_here, N2, D)
    d_three = jnp.einsum(
        "rsc,sp->crp", d_mix_cube, fourth_block, preferred_element_type=f32
    ).astype(bf16)
    d_freq = jnp.einsum(
        "crp,rq->cqp",
        lax.all_to_all(d_three, "seq", split_axis=0, concat_axis=1, tiled=True),
        third_block,
        preferred_element_type=f32,
    )
    grad_kernel = (d_freq * spectrum).astype(bf16)
    d_spec = (d_freq * kernel.astype(f32)).astype(bf16)
    d_one = jnp.einsum("cqp,qa->cap", d_spec, second_block, preferred_element_type=f32).astype(bf16)
    split_one = d_one.reshape(d_one.shape[0], n_devices, rows_here, N2)
    d_cube = jnp.einsum(
        "cap,pb->abc",
        lax.all_to_all(split_one, "seq", split_axis=1, concat_axis=0, tiled=True)[:, 0],
        first_block,
        preferred_element_type=f32,
    )
    d_value = (d_cube.reshape(local_rows, D) + skip_gain * d_mix.astype(f32)).astype(bf16)
    grad_tokens = (
        jnp.dot(d_value, w_value.T, preferred_element_type=f32)
        + jnp.dot(d_gate, w_gate.T, preferred_element_type=f32)
    ).astype(bf16)
    factor = 1.0 / jnp.sqrt(jnp.asarray(N1 * N2, f32))
    value_term = jnp.dot(tokens.T, d_value, preferred_element_type=f32) * factor
    gate_term = jnp.dot(tokens.T, d_gate, preferred_element_type=f32) * factor
    skip_term = jnp.sum(d_mix.astype(f32) * value.astype(f32), axis=0) * factor
    value_total, gate_total, skip_total = (
        lax.psum(value_term.astype(jnp.bfloat16), "seq").astype(jnp.float32),
        lax.psum(gate_term.astype(jnp.bfloat16), "seq").astype(jnp.float32),
        lax.psum(skip_term.astype(jnp.bfloat16), "seq").astype(jnp.float32),
    )
    return (grad_tokens, grad_kernel, jnp.stack([value_total, gate_total]), skip_total)


def solution(mesh):
    in_specs = (
        P(("parts", "seq"), None),
        P(),
        P(),
        P(),
        P(),
        P(),
        P(),
        P("seq", None, None),
        P(),
        P(("parts", "seq"), None),
    )
    out_specs = (
        P(("parts", "seq"), None),
        P(("parts", "seq"), None, None),
        P("parts", None, None),
        P("parts"),
    )
    return jax.shard_map(
        on_device, mesh=mesh, in_specs=in_specs, out_specs=out_specs, check_vma=False
    )
```

profile of v0, /device:TPU:0, one launch (start us, length us, event | category | flops | bytes accessed | tf_op | source)
XLA Modules:
  0.0 597.8 jit_solution(15915618487453710336)
XLA Ops:
  7.2 6.0 %fusion = bf16[4096,512]{1,0:T(8,128)(2,1)S(1)} fusion(bf16[4096,512]{1,0:T(8,128)(2,1)} %param.19, bf16[4096,512]{1,0:T(8,128)(2,1)} %param.10, bf16[512,512]{1,0:T(8,128)(2,1)} %param.12), kind=kOutput, calls=%fused_computation.7 | convolution fusion | flops 2157969408 | bytes 13107200 | tf_op jit(solution)/shard_map/dot_general | solution.py:29
  16.5 4.4 copy.60
  20.9 7.5 %all-to-all-start = ((bf16[512,16,256]{2,1,0:T(8,128)(2,1)}), bf16[512,16,256]{2,1,0:T(8,128)(2,1)}, u32[]{:S(2)}, u32[]{:S(2)}) async-start(bf16[512,16,256]{2,1,0:T(8,128)(2,1)} %copy.60), calls=%async_computation | async-start | bytes 8388608 | tf_op jit(solution)/shard_map/all_to_all | solution.py:61
  28.4 4.6 convolution_convert_fusion
  36.3 4.4 copy.70
  40.7 65.3 %all-to-all-done = bf16[512,16,256]{2,1,0:T(8,128)(2,1)} async-done(((bf16[512,16,256]{2,1,0:T(8,128)(2,1)}), bf16[512,16,256]{2,1,0:T(8,128)(2,1)}, u32[]{:S(2)}, u32[]{:S(2)}) %all-to-all-start) | async-done | bytes 4194336 | tf_op jit(solution)/shard_map/all_to_all | solution.py:61
  106.0 19.7 %all-to-all-start.2 = ((bf16[512,16,256]{2,1,0:T(8,128)(2,1)}), bf16[512,16,256]{2,1,0:T(8,128)(2,1)}, u32[]{:S(2)}, u32[]{:S(2)}) async-start(bf16[512,16,256]{2,1,0:T(8,128)(2,1)} %copy.70), calls=%async_computation.2 | async-start | bytes 8388608 | tf_op jit(solution)/shard_map/all_to_all | solution.py:36
  125.7 6.4 %copy.63 = bf16[32,256,256]{1,2,0:T(8,128)(2,1)} copy(bf16[32,256,256]{2,1,0:T(8,128)(2,1)} %param.17) | data formatting | bytes 8388608 | tf_op args[7]
  132.1 4.7 copy.61
  136.8 66.4 %all-to-all-done.2 = bf16[512,16,256]{2,1,0:T(8,128)(2,1)} async-done(((bf16[512,16,256]{2,1,0:T(8,128)(2,1)}), bf16[512,16,256]{2,1,0:T(8,128)(2,1)}, u32[]{:S(2)}, u32[]{:S(2)}) %all-to-all-start.2) | async-done | bytes 4194336 | tf_op jit(solution)/shard_map/all_to_all | solution.py:36
  217.3 19.7 %all-to-all-start.3 = ((bf16[32,16,16,256]{3,2,0,1:T(8,128)(2,1)}), bf16[32,16,16,256]{3,2,0,1:T(8,128)(2,1)}, u32[]{:S(2)}, u32[]{:S(2)}) async-start(bf16[32,16,16,256]{3,2,0,1:T(8,128)(2,1)} %copy.74), calls=%async_computation.3 | async-start | bytes 8388608 | tf_op jit(solution)/shard_map/all_to_all | solution.py:47
  237.0 6.0 fusion.13
  245.4 69.2 %all-to-all-done.3 = bf16[32,16,16,256]{3,2,0,1:T(8,128)(2,1)} async-done(((bf16[32,16,16,256]{3,2,0,1:T(8,128)(2,1)}), bf16[32,16,16,256]{3,2,0,1:T(8,128)(2,1)}, u32[]{:S(2)}, u32[]{:S(2)}) %all-to-all-start.3) | async-done | bytes 4194336 | tf_op jit(solution)/shard_map/all_to_all | solution.py:47
  314.6 19.7 %all-to-all-start.1 = ((bf16[32,16,16,256]{3,2,0,1:T(8,128)(2,1)}), bf16[32,16,16,256]{3,2,0,1:T(8,128)(2,1)}, u32[]{:S(2)}, u32[]{:S(2)}) async-start(bf16[32,16,16,256]{3,2,0,1:T(8,128)(2,1)} %copy.66), calls=%async_computation.1 | async-start | bytes 8388608 | tf_op jit(solution)/shard_map/all_to_all | solution.py:71
  334.3 6.4 %copy.76 = bf16[32,256,256]{2,1,0:T(8,128)(2,1)} copy(bf16[32,256,256]{1,2,0:T(8,128)(2,1)} %get-tuple-element.25) | data formatting | bytes 8388608
  344.4 4.5 fusion.32
  348.9 62.9 %all-to-all-done.1 = bf16[32,16,16,256]{3,2,0,1:T(8,128)(2,1)} async-done(((bf16[32,16,16,256]{3,2,0,1:T(8,128)(2,1)}), bf16[32,16,16,256]{3,2,0,1:T(8,128)(2,1)}, u32[]{:S(2)}, u32[]{:S(2)}) %all-to-all-start.1) | async-done | bytes 4194336 | tf_op jit(solution)/shard_map/all_to_all | solution.py:71
  415.7 4.5 fusion.24
  420.2 10.9 %fusion.7 = (f32[512]{0:T(512)S(1)}, bf16[4096,512]{1,0:T(8,128)(2,1)}, bf16[4096,512]{1,0:T(8,128)(2,1)S(1)}) fusion(bf16[4096,512]{1,0:T(8,128)(2,1)} %copy-done.6, bf16[4096,512]{1,0:T(8,128)(2,1)} %copy-done.5, f32[512]{0:T(512)S(1)} %copy-done.13, f32[512,16,256]{0,2,1:T(8,128)} %fusion.24, f32[512,16,256]{0,2,1:T(8,128)S(1)} %bitcast.101, ...), kind=kLoop, calls=%fused_computation.14 | loop fusion | flops 25165312 | bytes 37752832 | tf_op jit(solution)/shard_map/reduce_sum | solution.py:83
  431.0 8.2 %fusion.22 = bf16[1,512,512]{1,2,0:T(8,128)(2,1)} fusion(bf16[4096,512]{1,0:T(8,128)(2,1)} %get-tuple-element.23, bf16[4096,512]{1,0:T(8,128)(2,1)} %param.10), kind=kOutput, calls=%fused_computation.31 | convolution fusion | flops 2148007936 | bytes 8912896 | tf_op jit(solution)/shard_map/dot_general | solution.py:81
  439.2 5.9 fusion.35
  448.3 47.8 %psum.23 = bf16[512]{0:T(512)(128)(2,1)S(1)} all-reduce(bf16[512]{0:T(512)(128)(2,1)S(1)} %multiply_convert_fusion), channel_id=1, replica_groups=mesh['parts'=2,'seq'=16] {'seq'}, use_global_device_ids=true, to_apply=%region_3.0 | all-reduce | flops 512 | bytes 2048 | tf_op jit(solution)/shard_map/psum | solution.py:87
  496.6 9.2 %add_convert_fusion = bf16[4096,512]{1,0:T(8,128)(2,1)} fusion(f32[4096,512]{1,0:T(8,128)} %fusion.35, bf16[4096,512]{1,0:T(8,128)(2,1)} %copy-done.3, bf16[512,512]{1,0:T(8,128)(2,1)S(1)} %copy-done.12), kind=kOutput, calls=%fused_computation.17 | convolution fusion | flops 2151677952 | bytes 17301504 | tf_op jit(solution)/shard_map/dot_general | solution.py:78
  505.8 82.0 %all-reduce.3.cloned.1.call-done = (bf16[1,512,512]{1,2,0:T(8,128)(2,1)}, bf16[1,512,512]{1,2,0:T(8,128)(2,1)}) async-done(((bf16[1,512,512]{1,2,0:T(8,128)(2,1)}, bf16[1,512,512]{1,2,0:T(8,128)(2,1)}), (bf16[1,512,512]{1,2,0:T(8,128)(2,1)}, bf16[1,512,512]{1,2,0:T(8,128)(2,1)})) %all-reduce.3.cloned.1.call-update) | async-done | bytes 1048592 | tf_op jit(solution)/shard_map/psum | solution.py:86
  (52 shorter events, 37.5 us)
Async XLA Ops:
  7.2 21.3 %copy-start = (bf16[512,512]{1,0:T(8,128)(2,1)S(1)}, bf16[512,512]{1,0:T(8,128)(2,1)}, u32[]{:S(2)}) copy-start(bf16[512,512]{1,0:T(8,128)(2,1)} %param.11) | copy-start | bytes 1572868
  7.2 8.0 %copy-start.10 = (bf16[256,256]{1,0:T(8,128)(2,1)S(1)}, bf16[256,256]{1,0:T(8,128)(2,1)}, u32[]{:S(2)}) copy-start(bf16[256,256]{1,0:T(8,128)(2,1)} %param.16) | copy-start | bytes 393220
  13.2 1.9 copy-start.5
  20.9 85.0 %all-to-all-start = ((bf16[512,16,256]{2,1,0:T(8,128)(2,1)}), bf16[512,16,256]{2,1,0:T(8,128)(2,1)}, u32[]{:S(2)}, u32[]{:S(2)}) async-start(bf16[512,16,256]{2,1,0:T(8,128)(2,1)} %copy.60), calls=%async_computation | async-start | bytes 8388608 | tf_op jit(solution)/shard_map/all_to_all | solution.py:61
  28.4 6.6 %copy-start.11 = (bf16[256,256]{1,0:T(8,128)(2,1)S(1)}, bf16[256,256]{1,0:T(8,128)(2,1)}, u32[]{:S(2)}) copy-start(bf16[256,256]{1,0:T(8,128)(2,1)} %param.13) | copy-start | bytes 393220
  33.0 2.0 copy-start.6
  106.0 97.2 %all-to-all-start.2 = ((bf16[512,16,256]{2,1,0:T(8,128)(2,1)}), bf16[512,16,256]{2,1,0:T(8,128)(2,1)}, u32[]{:S(2)}, u32[]{:S(2)}) async-start(bf16[512,16,256]{2,1,0:T(8,128)(2,1)} %copy.70), calls=%async_computation.2 | async-start | bytes 8388608 | tf_op jit(solution)/shard_map/all_to_all | solution.py:36
  203.2 3.4 copy-start.7
  203.2 3.5 copy-start.8
  206.6 1.3 copy-start.9
  208.0 5.6 copy-start.1
  208.0 5.6 copy-start.2
  217.3 97.3 %all-to-all-start.3 = ((bf16[32,16,16,256]{3,2,0,1:T(8,128)(2,1)}), bf16[32,16,16,256]{3,2,0,1:T(8,128)(2,1)}, u32[]{:S(2)}, u32[]{:S(2)}) async-start(bf16[32,16,16,256]{3,2,0,1:T(8,128)(2,1)} %copy.74), calls=%async_computation.3 | async-start | bytes 8388608 | tf_op jit(solution)/shard_map/all_to_all | solution.py:47
  314.6 97.2 %all-to-all-start.1 = ((bf16[32,16,16,256]{3,2,0,1:T(8,128)(2,1)}), bf16[32,16,16,256]{3,2,0,1:T(8,128)(2,1)}, u32[]{:S(2)}, u32[]{:S(2)}) async-start(bf16[32,16,16,256]{3,2,0,1:T(8,128)(2,1)} %copy.66), calls=%async_computation.1 | async-start | bytes 8388608 | tf_op jit(solution)/shard_map/all_to_all | solution.py:71
  334.3 253.5 %all-reduce.3.cloned.1.call-start = ((), (), s32[]{:S(2)}) async-start(), calls=%async_computation.4 | async-start | bytes 2097152 | tf_op jit(solution)/shard_map/psum | solution.py:86
  411.8 8.3 %slice-start = ((s8[8388608]{0:T(1024)(128)(4,1)}), s8[4194304]{0:T(1024)(128)(4,1)S(1)}, s32[]{:S(2)}) async-start(s8[8388608]{0:T(1024)(128)(4,1)} %bitcast.100), calls=%async_computation.5 | async-start | bytes 8388608
  415.6 4.5 slice-start.1
  415.6 4.5 copy-start.13
  431.0 14.1 %copy-start.3 = (bf16[4096,512]{1,0:T(8,128)(2,1)}, bf16[4096,512]{1,0:T(8,128)(2,1)S(1)}, u32[]{:S(2)}) copy-start(bf16[4096,512]{1,0:T(8,128)(2,1)S(1)} %get-tuple-element.24) | copy-start | bytes 12582916
  431.0 8.2 %copy-start.4 = (bf16[4096,512]{1,0:T(8,128)(2,1)S(1)}, bf16[4096,512]{1,0:T(8,128)(2,1)}, u32[]{:S(2)}) copy-start(bf16[4096,512]{1,0:T(8,128)(2,1)} %get-tuple-element.23) | copy-start | bytes 12582916
  439.2 5.9 copy-start.14
  445.1 51.5 %copy-start.12 = (bf16[512,512]{1,0:T(8,128)(2,1)S(1)}, bf16[512,512]{1,0:T(8,128)(2,1)}, u32[]{:S(2)}) copy-start(bf16[512,512]{1,0:T(8,128)(2,1)} %param.12) | copy-start | bytes 1572868
Sparse Core Ops, SparseCore 0:
  496.8 90.9 all-reduce.2
where the time goes:
time: 599 us; the launch traced here: 598 us
  waiting for transfers between devices  346 us (58%)
  starting transfers between devices  66.6 us (11%)
  matrix products  60.6 us (10%)
  local copies, waits for them, and re-layouts  50.1 us (8%)
  blocking collectives  47.8 us (8%)
  between operations  14.3 us (2%)
  other arithmetic  12.8 us (2%)
    psum x1, waiting for transfers between devices, on_device(): lax.psum(gate_term.astype(jnp.bfloat16), 'seq').astype(jnp.float32)  82 us
    all_to_all x1, waiting for transfers between devices, on_device(): lax.all_to_all(split_three, 'seq', split_axis=1, concat_axis=0, tiled=True)  69.2 us
    all_to_all x1, waiting for transfers between devices, on_device(): lax.all_to_all(section_one, 'seq', split_axis=0, concat_axis=1, tiled=True)  66.4 us
    all_to_all x1, waiting for transfers between devices, on_device(): lax.all_to_all(d_three, 'seq', split_axis=0, concat_axis=1, tiled=True)  65.3 us
    all_to_all x1, waiting for transfers between devices, on_device(): lax.all_to_all(split_one, 'seq', split_axis=1, concat_axis=0, tiled=True)  62.9 us
    psum x1, blocking collectives, on_device(): lax.psum(skip_term.astype(jnp.bfloat16), 'seq').astype(jnp.float32)  47.8 us
    unnamed x37, local copies, waits for them, and re-layouts  21.5 us
    all_to_all x1, starting transfers between devices, on_device(): lax.all_to_all(split_three, 'seq', split_axis=1, concat_axis=0, tiled=True)  19.7 us
  transfers between devices with their start and end apart: 5, of which 5 were waited for; matrix products, arithmetic and copies ran while one was open for 9% of the time, Pallas kernels for 0%

commit v1 on v0

--- a/solution.py
+++ b/solution.py
@@ -68,7 +68,12 @@
     split_one = d_one.reshape(d_one.shape[0], n_devices, rows_here, N2)
     d_cube = jnp.einsum(
         "cap,pb->abc",
-        lax.all_to_all(split_one, "seq", split_axis=1, concat_axis=0, tiled=True)[:, 0],
+        jnp.concatenate(
+            lax.all_to_all(
+                jnp.stack(jnp.split(split_one, lax.axis_size("seq"), axis=1)), "seq", 0, 0
+            ),
+            axis=0,
+        )[:, 0],
         first_block,
         preferred_element_type=f32,
     )

time: 599 us -> 582 us (0.972)
  waiting for transfers between devices: 346 us -> 325 us
  local copies, waits for them, and re-layouts: 50.1 us -> 57.1 us
    all_to_all x1, waiting for transfers between devices: 66.4 us -> 51.2 us  [on_device(): lax.all_to_all(section_one, 'seq', split_axis=0, concat_axis=1, tiled=True)]
    unnamed x37 -> x42, local copies, waits for them, and re-layouts: 21.5 us -> 32.3 us
    all_to_all x1, waiting for transfers between devices: 69.2 us -> 62.7 us  [on_device(): lax.all_to_all(split_three, 'seq', split_axis=1, concat_axis=0, tiled=True)]
  transfers between devices with their start and end apart: 5 -> 5, of which waited for: 5 -> 5; matrix products, arithmetic and copies ran while one was open for 9% -> 12% of each run, Pallas kernels for 0% -> 0%
where the time goes in v1:
time: 582 us; the launch traced here: 581 us
  waiting for transfers between devices  325 us (56%)
  starting transfers between devices  66.8 us (11%)
  local copies, waits for them, and re-layouts  57.1 us (10%)
  matrix products  56.6 us (10%)
  blocking collectives  48 us (8%)
  between operations  14.3 us (2%)
  other arithmetic  12.9 us (2%)
    psum x1, waiting for transfers between devices, on_device(): lax.psum(gate_term.astype(jnp.bfloat16), 'seq').astype(jnp.float32)  82 us
    all_to_all x1, waiting for transfers between devices, on_device(): lax.all_to_all(d_three, 'seq', split_axis=0, concat_axis=1, tiled=True)  65.2 us
    all_to_all x1, waiting for transfers between devices, on_device(): lax.all_to_all(jnp.stack(jnp.split(split_one, lax.axis_size('seq'), axis=...  64.3 us
    all_to_all x1, waiting for transfers between devices, on_device(): lax.all_to_all(split_three, 'seq', split_axis=1, concat_axis=0, tiled=True)  62.7 us
    all_to_all x1, waiting for transfers between devices, on_device(): lax.all_to_all(section_one, 'seq', split_axis=0, concat_axis=1, tiled=True)  51.2 us
    psum x1, blocking collectives, on_device(): lax.psum(skip_term.astype(jnp.bfloat16), 'seq').astype(jnp.float32)  48 us
    unnamed x42, local copies, waits for them, and re-layouts  32.3 us
    all_to_all x1, starting transfers between devices, on_device(): lax.all_to_all(section_one, 'seq', split_axis=0, concat_axis=1, tiled=True)  19.7 us
  transfers between devices with their start and end apart: 5, of which 5 were waited for; matrix products, arithmetic and copies ran while one was open for 12% of the time, Pallas kernels for 0%

profile of v1, /device:TPU:0, one launch (start us, length us, event | category | flops | bytes accessed | tf_op | source)
XLA Modules:
  0.0 581.1 jit_solution(18249086286279025760)
XLA Ops:
  7.2 6.0 %fusion = bf16[4096,512]{1,0:T(8,128)(2,1)S(1)} fusion(bf16[4096,512]{1,0:T(8,128)(2,1)} %param.19, bf16[4096,512]{1,0:T(8,128)(2,1)} %param.10, bf16[512,512]{1,0:T(8,128)(2,1)} %param.12), kind=kOutput, calls=%fused_computation.7 | convolution fusion | flops 2157969408 | bytes 13107200 | tf_op jit(solution)/shard_map/dot_general | solution.py:29
  16.5 4.4 copy.104
  20.9 7.5 %all-to-all-start = ((bf16[512,16,256]{2,1,0:T(8,128)(2,1)}), bf16[512,16,256]{2,1,0:T(8,128)(2,1)}, u32[]{:S(2)}, u32[]{:S(2)}) async-start(bf16[512,16,256]{2,1,0:T(8,128)(2,1)} %copy.104), calls=%async_computation | async-start | bytes 8388608 | tf_op jit(solution)/shard_map/all_to_all | solution.py:61
  28.5 4.6 convolution_convert_fusion
  36.4 4.4 copy.128
  40.8 65.2 %all-to-all-done = bf16[512,16,256]{2,1,0:T(8,128)(2,1)} async-done(((bf16[512,16,256]{2,1,0:T(8,128)(2,1)}), bf16[512,16,256]{2,1,0:T(8,128)(2,1)}, u32[]{:S(2)}, u32[]{:S(2)}) %all-to-all-start) | async-done | bytes 4194336 | tf_op jit(solution)/shard_map/all_to_all | solution.py:61
  106.0 19.7 %all-to-all-start.2 = ((bf16[512,16,256]{2,1,0:T(8,128)(2,1)}), bf16[512,16,256]{2,1,0:T(8,128)(2,1)}, u32[]{:S(2)}, u32[]{:S(2)}) async-start(bf16[512,16,256]{2,1,0:T(8,128)(2,1)} %copy.128), calls=%async_computation.2 | async-start | bytes 8388608 | tf_op jit(solution)/shard_map/all_to_all | solution.py:36
  125.7 6.4 %copy.107 = bf16[32,256,256]{1,2,0:T(8,128)(2,1)} copy(bf16[32,256,256]{2,1,0:T(8,128)(2,1)} %param.17) | data formatting | bytes 8388608 | tf_op args[7]
  152.0 51.2 %all-to-all-done.2 = bf16[512,16,256]{2,1,0:T(8,128)(2,1)} async-done(((bf16[512,16,256]{2,1,0:T(8,128)(2,1)}), bf16[512,16,256]{2,1,0:T(8,128)(2,1)}, u32[]{:S(2)}, u32[]{:S(2)}) %all-to-all-start.2) | async-done | bytes 4194336 | tf_op jit(solution)/shard_map/all_to_all | solution.py:36
  203.2 19.7 %all-to-all-start.1 = ((bf16[16,32,1,16,256]{4,3,1,2,0:T(8,128)(2,1)}), bf16[16,32,1,16,256]{4,3,1,2,0:T(8,128)(2,1)}, u32[]{:S(2)}, u32[]{:S(2)}) async-start(bf16[16,32,1,16,256]{4,3,1,2,0:T(8,128)(2,1)} %fusion.23), calls=%async_computation.1 | async-start | bytes 8388608 | tf_op jit(solution)/shard_map/all_to_all | solution.py:72
  225.7 6.8 %fusion.8 = (bf16[32,256,256]{1,2,0:T(8,128)(2,1)}, f32[32,256,256]{2,1,0:T(8,128)S(1)}) fusion(f32[32,256,256]{2,1,0:T(8,128)} %copy-done.1, bf16[32,256,256]{2,1,0:T(8,128)(2,1)S(1)} %bitcast.212, bf16[256,256]{1,0:T(8,128)(2,1)S(1)} %copy-done.6), kind=kOutput, calls=%fused_computation.16 | convolution fusion | flops 1077936128 | bytes 25296896 | tf_op jit(solution)/shard_map/cap,qa->cqp/dot_general | solution.py:34
  236.2 64.3 %all-to-all-done.1 = bf16[16,32,1,16,256]{4,3,1,2,0:T(8,128)(2,1)} async-done(((bf16[16,32,1,16,256]{4,3,1,2,0:T(8,128)(2,1)}), bf16[16,32,1,16,256]{4,3,1,2,0:T(8,128)(2,1)}, u32[]{:S(2)}, u32[]{:S(2)}) %all-to-all-start.1) | async-done | bytes 4194336 | tf_op jit(solution)/shard_map/all_to_all | solution.py:72
  300.5 19.7 %all-to-all-start.3 = ((bf16[32,16,16,256]{3,2,0,1:T(8,128)(2,1)}), bf16[32,16,16,256]{3,2,0,1:T(8,128)(2,1)}, u32[]{:S(2)}, u32[]{:S(2)}) async-start(bf16[32,16,16,256]{3,2,0,1:T(8,128)(2,1)} %copy.132), calls=%async_computation.3 | async-start | bytes 8388608 | tf_op jit(solution)/shard_map/all_to_all | solution.py:47
  320.4 6.4 %copy.134 = bf16[32,256,256]{2,1,0:T(8,128)(2,1)} copy(bf16[32,256,256]{1,2,0:T(8,128)(2,1)} %get-tuple-element.25) | data formatting | bytes 8388608
  330.5 4.5 fusion.40
  335.0 62.7 %all-to-all-done.3 = bf16[32,16,16,256]{3,2,0,1:T(8,128)(2,1)} async-done(((bf16[32,16,16,256]{3,2,0,1:T(8,128)(2,1)}), bf16[32,16,16,256]{3,2,0,1:T(8,128)(2,1)}, u32[]{:S(2)}, u32[]{:S(2)}) %all-to-all-start.3) | async-done | bytes 4194336 | tf_op jit(solution)/shard_map/all_to_all | solution.py:47
  397.7 3.7 copy.133
  402.7 10.9 %fusion.7 = (f32[512]{0:T(512)S(1)}, bf16[4096,512]{1,0:T(8,128)(2,1)S(1)}, bf16[4096,512]{1,0:T(8,128)(2,1)}) fusion(bf16[4096,512]{1,0:T(8,128)(2,1)} %copy-done.5, bf16[4096,512]{1,0:T(8,128)(2,1)} %copy-done.4, f32[512]{0:T(512)S(1)} %copy-done.11, f32[512,16,256]{0,2,1:T(8,128)} %fusion.40, f32[512,16,256]{0,2,1:T(8,128)S(1)} %fusion.48, ...), kind=kLoop, calls=%fused_computation.14 | loop fusion | flops 25165312 | bytes 37752832 | tf_op jit(solution)/shard_map/reduce_sum | solution.py:88
  413.6 5.3 fusion.22
  419.0 5.6 fusion.51
  424.6 48.0 %psum.23 = bf16[512]{0:T(512)(128)(2,1)S(1)} all-reduce(bf16[512]{0:T(512)(128)(2,1)S(1)} %multiply_convert_fusion), channel_id=1, replica_groups=mesh['parts'=2,'seq'=16] {'seq'}, use_global_device_ids=true, to_apply=%region_3.0 | all-reduce | flops 512 | bytes 2048 | tf_op jit(solution)/shard_map/psum | solution.py:92
  473.2 6.7 %fusion.21 = bf16[1,512,512]{1,2,0:T(8,128)(2,1)} fusion(bf16[4096,512]{1,0:T(8,128)(2,1)} %get-tuple-element.24, bf16[4096,512]{1,0:T(8,128)(2,1)} %param.10), kind=kOutput, calls=%fused_computation.30 | convolution fusion | flops 2148007936 | bytes 8912896 | tf_op jit(solution)/shard_map/dot_general | solution.py:87
  479.9 9.2 %add_convert_fusion = bf16[4096,512]{1,0:T(8,128)(2,1)} fusion(f32[4096,512]{1,0:T(8,128)} %fusion.51, bf16[4096,512]{1,0:T(8,128)(2,1)} %get-tuple-element.24, bf16[512,512]{1,0:T(8,128)(2,1)S(1)} %copy-done.10), kind=kOutput, calls=%fused_computation.17 | convolution fusion | flops 2151677952 | bytes 17301504 | tf_op jit(solution)/shard_map/dot_general | solution.py:83
  489.1 82.0 %all-reduce.3.cloned.1.call-done = (bf16[1,512,512]{1,2,0:T(8,128)(2,1)}, bf16[1,512,512]{1,2,0:T(8,128)(2,1)}) async-done(((bf16[1,512,512]{1,2,0:T(8,128)(2,1)}, bf16[1,512,512]{1,2,0:T(8,128)(2,1)}), (bf16[1,512,512]{1,2,0:T(8,128)(2,1)}, bf16[1,512,512]{1,2,0:T(8,128)(2,1)})) %all-reduce.3.cloned.1.call-update) | async-done | bytes 1048592 | tf_op jit(solution)/shard_map/psum | solution.py:91
  (56 shorter events, 41.9 us)
Async XLA Ops:
  7.2 21.3 %copy-start = (bf16[512,512]{1,0:T(8,128)(2,1)S(1)}, bf16[512,512]{1,0:T(8,128)(2,1)}, u32[]{:S(2)}) copy-start(bf16[512,512]{1,0:T(8,128)(2,1)} %param.11) | copy-start | bytes 1572868
  7.2 8.0 %copy-start.9 = (bf16[256,256]{1,0:T(8,128)(2,1)S(1)}, bf16[256,256]{1,0:T(8,128)(2,1)}, u32[]{:S(2)}) copy-start(bf16[256,256]{1,0:T(8,128)(2,1)} %param.16) | copy-start | bytes 393220
  13.2 2.0 copy-start.4
  20.9 85.0 %all-to-all-start = ((bf16[512,16,256]{2,1,0:T(8,128)(2,1)}), bf16[512,16,256]{2,1,0:T(8,128)(2,1)}, u32[]{:S(2)}, u32[]{:S(2)}) async-start(bf16[512,16,256]{2,1,0:T(8,128)(2,1)} %copy.104), calls=%async_computation | async-start | bytes 8388608 | tf_op jit(solution)/shard_map/all_to_all | solution.py:61
  28.4 6.6 %copy-start.8 = (bf16[256,256]{1,0:T(8,128)(2,1)S(1)}, bf16[256,256]{1,0:T(8,128)(2,1)}, u32[]{:S(2)}) copy-start(bf16[256,256]{1,0:T(8,128)(2,1)} %param.13) | copy-start | bytes 393220
  33.0 2.0 copy-start.5
  106.0 97.2 %all-to-all-start.2 = ((bf16[512,16,256]{2,1,0:T(8,128)(2,1)}), bf16[512,16,256]{2,1,0:T(8,128)(2,1)}, u32[]{:S(2)}, u32[]{:S(2)}) async-start(bf16[512,16,256]{2,1,0:T(8,128)(2,1)} %copy.128), calls=%async_computation.2 | async-start | bytes 8388608 | tf_op jit(solution)/shard_map/all_to_all | solution.py:36
  132.1 2.8 copy-start.7
  134.9 2.2 copy-start.2
  134.9 2.2 copy-start.6
  137.1 3.2 copy-start.1
  203.2 97.2 %all-to-all-start.1 = ((bf16[16,32,1,16,256]{4,3,1,2,0:T(8,128)(2,1)}), bf16[16,32,1,16,256]{4,3,1,2,0:T(8,128)(2,1)}, u32[]{:S(2)}, u32[]{:S(2)}) async-start(bf16[16,32,1,16,256]{4,3,1,2,0:T(8,128)(2,1)} %fusion.23), calls=%async_computation.1 | async-start | bytes 8388608 | tf_op jit(solution)/shard_map/all_to_all | solution.py:72
  225.7 6.8 %copy-start.3 = (bf16[32,256,256]{1,2,0:T(8,128)(2,1)S(1)}, bf16[32,256,256]{1,2,0:T(8,128)(2,1)}, u32[]{:S(2)}) copy-start(bf16[32,256,256]{1,2,0:T(8,128)(2,1)} %copy.107) | copy-start | bytes 12582916
  300.5 97.2 %all-to-all-start.3 = ((bf16[32,16,16,256]{3,2,0,1:T(8,128)(2,1)}), bf16[32,16,16,256]{3,2,0,1:T(8,128)(2,1)}, u32[]{:S(2)}, u32[]{:S(2)}) async-start(bf16[32,16,16,256]{3,2,0,1:T(8,128)(2,1)} %copy.132), calls=%async_computation.3 | async-start | bytes 8388608 | tf_op jit(solution)/shard_map/all_to_all | solution.py:47
  320.2 250.9 %all-reduce.3.cloned.1.call-start = ((), (), s32[]{:S(2)}) async-start(), calls=%async_computation.4 | async-start | bytes 2097152 | tf_op jit(solution)/shard_map/psum | solution.py:91
  401.4 1.3 copy-start.11
  473.2 6.7 %copy-start.10 = (bf16[512,512]{1,0:T(8,128)(2,1)S(1)}, bf16[512,512]{1,0:T(8,128)(2,1)}, u32[]{:S(2)}) copy-start(bf16[512,512]{1,0:T(8,128)(2,1)} %param.12) | copy-start | bytes 1572868
Sparse Core Ops, SparseCore 0:
  480.0 91.0 all-reduce.2
